TPU v7x, 128 devices: a whole 4x4x4 slice. The times are simulated.
128 devices in a mesh: leaf: 4 (over y), row: 4 (over z), col: 8 (over x, core).
Axes of the slice: x: 4, y: 4, z: 4, core: 2. Of those that a mesh axis runs over, the one named last changes fastest.
Arguments:
- rhs_leaf: bfloat16 [4, 12288, 256], P('leaf', 'col'), may hold values from -6 to 6
- rhs_parent: bfloat16 [16384, 256], P(('leaf', 'row', 'col')), may hold values from -6 to 6
- inv_leaf: bfloat16 [4, 12288, 12288], P('leaf', 'row', 'col'), as said below
- panel: bfloat16 [4, 6144, 12288], P('leaf', 'col', 'row'), may hold values from -0.0546875 to 0.0546875
- row_map: int32 [4, 6144], P('leaf', 'col'), may hold values from 0 to 16383, as said below
- inv_parent: bfloat16 [16384, 16384], P(('row', 'col'), 'leaf'), as said below
Outputs:
- sol_leaf: bfloat16 [4, 12288, 256], P('leaf', 'col')
- sol_parent: bfloat16 [16384, 256], P(('leaf', 'row', 'col'))
Inputs may be any that keep to these rules, and one draw needn't show every extreme that they name: Within one leaf the 6144 entries of row_map are distinct parent rows. Split the parent rows into 128 owner blocks of 16384 // 128 consecutive rows: in each aligned block of 192 consecutive entries of a leaf, at most 2 entries fall in one owner block, and exactly 2 in some. `inv_leaf`: lower triangular: zeros above the diagonal, diagonal entries between 0.5 and 2. `inv_parent`: lower triangular: zeros above the diagonal, diagonal entries between 0.5 and 2.
All inputs are finite; a program needn't handle non-finite values.
Results may differ from a plain program's by a relative error of at most 0.01.
Values may be sent and summed in bfloat16 or wider, within the bound.
A program may use at most 128 MiB of HBM per device.

v0:
```python
import jax
import jax.numpy as jnp
from jax import lax
from jax.sharding import PartitionSpec as P


def dense_updates(update, row_map, rhs_parent):
    total_rows = rhs_parent.shape[0] * lax.axis_size(("leaf", "row", "col"))
    dense = jnp.zeros((total_rows, rhs_parent.shape[1]), jnp.float32)
    dense = dense.at[row_map[0]].add(-update)
    offset = lax.axis_index(("leaf", "row", "col")) * rhs_parent.shape[0]
    own_rows = lax.dynamic_slice_in_dim(dense, offset, rhs_parent.shape[0], 0) + rhs_parent.astype(
        jnp.float32
    )
    return lax.dynamic_update_slice_in_dim(dense, own_rows, offset, 0)


def per_device(rhs_leaf, rhs_parent, inv_leaf, panel, row_map, inv_parent):
    leaf_part = jnp.dot(inv_leaf[0], rhs_leaf[0], preferred_element_type=jnp.float32)
    forward = lax.psum(leaf_part, "col").astype(jnp.bfloat16)
    update = jnp.dot(panel[0], forward, preferred_element_type=jnp.float32)
    dense = dense_updates(update, row_map, rhs_parent)
    leaf_block = lax.psum_scatter(dense, "leaf", scatter_dimension=0, tiled=True)
    reduced = lax.psum(leaf_block, ("row", "col")).astype(jnp.bfloat16)
    parent_part = jnp.dot(inv_parent, reduced, preferred_element_type=jnp.float32)
    fwd_parent = lax.psum(parent_part, "leaf").astype(jnp.bfloat16)
    back_part = lax.dot_general(
        inv_parent, fwd_parent, (((0,), (0,)), ((), ())), preferred_element_type=jnp.float32
    )
    sol_parent = lax.psum_scatter(
        back_part, ("row", "col"), scatter_dimension=0, tiled=True
    ).astype(jnp.bfloat16)
    whole_parent = lax.all_gather(sol_parent, ("leaf", "row", "col"), axis=0, tiled=True)
    picked = jnp.take(whole_parent, row_map[0], axis=0)
    coupling_part = lax.dot_general(
        panel[0], picked, (((0,), (0,)), ((), ())), preferred_element_type=jnp.float32
    )
    coupling = lax.psum(coupling_part, "col")
    corrected = (forward.astype(jnp.float32) - coupling).astype(jnp.bfloat16)
    final_part = lax.dot_general(
        inv_leaf[0], corrected, (((0,), (0,)), ((), ())), preferred_element_type=jnp.float32
    )
    sol_leaf = lax.psum(final_part, "row").astype(jnp.bfloat16)
    return (sol_leaf[None], sol_parent)


def solution(mesh):
    in_specs = (
        P("leaf", "col", None),
        P(("leaf", "row", "col"), None),
        P("leaf", "row", "col"),
        P("leaf", "col", "row"),
        P("leaf", "col"),
        P(("row", "col"), "leaf"),
    )
    out_specs = (P("leaf", "col", None), P(("leaf", "row", "col"), None))
    return jax.shard_map(
        per_device, mesh=mesh, in_specs=in_specs, out_specs=out_specs, check_vma=False
    )
```

profile of v0, /device:TPU:0, one launch (start us, length us, event | category | flops | bytes accessed | tf_op | source)
XLA Modules:
  0.0 728.7 jit_solution(5863380692495050478)
XLA Ops:
  7.2 0.0 copy-start
  7.2 0.0 reduce-scatter.3.cloned.1.call-start
  7.2 1.1 copy-done
  8.3 8.0 %fusion.2 = f32[3072,256]{1,0:T(8,128)} fusion(bf16[1,3072,1536]{2,1,0:T(8,128)(2,1)} %param.8, bf16[1,1536,256]{2,1,0:T(8,128)(2,1)S(1)} %copy-done), kind=kOutput, calls=%fused_computation.4 | convolution fusion | flops 2415919104 | bytes 13369344 | tf_op jit(solution)/shard_map/dot_general | solution.py:19
  16.3 56.8 %all-reduce.7 = bf16[3072,256]{1,0:T(8,128)(2,1)S(1)} all-reduce(f32[3072,256]{1,0:T(8,128)} %fusion.2), channel_id=1, replica_groups=mesh['leaf'=4,'row'=4,'col'=8] {'col'}, use_global_device_ids=true, to_apply=%region_0.0 | all-reduce | flops 786432 | bytes 4718592 | tf_op jit(solution)/shard_map/psum | solution.py:20
  73.1 3.8 fusion.21
  76.9 0.3 copy.12
  77.2 12.3 %scatter_custom_fusion = f32[16384,256]{1,0:T(8,128)} fusion(s32[768]{0:T(1024)S(1)} %fusion.34, f32[768,256]{1,0:T(8,128)S(1)} %copy.12, f32[]{:T(128)} %constant.14.clone.1), kind=kCustom, calls=%fused_computation.6 | custom fusion | flops 196608 | bytes 16777220 | tf_op jit(solution)/shard_map/scatter-add | solution.py:10
  89.5 1.6 add_dynamic-update-slice_fusion
  91.0 0.0 reduce-scatter.3.cloned.1.call-update
  91.0 0.0 reduce-scatter.5.cloned.1.call-start
  91.1 148.2 %reduce-scatter.3.cloned.1.call-done = f32[4096,256]{1,0:T(8,128)} async-done(((f32[16384,256]{1,0:T(8,128)}), f32[4096,256]{1,0:T(8,128)}) %reduce-scatter.3.cloned.1.call-update) | async-done | bytes 4194320 | tf_op jit(solution)/shard_map/reduce_scatter | solution.py:23
  239.3 153.3 %all-reduce.8 = bf16[4096,256]{1,0:T(8,128)(2,1)} all-reduce(f32[4096,256]{1,0:T(8,128)} %reduce-scatter.3.cloned.1.call-done), channel_id=1, replica_groups=mesh['leaf'=4,'row'=4,'col'=8] {'row','col'}, use_global_device_ids=true, to_apply=%region_3.0 | all-reduce | flops 1048576 | bytes 6291456 | tf_op jit(solution)/shard_map/psum | solution.py:24
  392.6 4.1 fusion.24
  396.8 20.8 %all-reduce.9 = bf16[512,256]{0,1:T(8,128)(2,1)S(1)} all-reduce(f32[512,256]{0,1:T(8,128)S(1)} %fusion.24), channel_id=1, replica_groups=mesh['leaf'=4,'row'=4,'col'=8] {'leaf'}, use_global_device_ids=true, to_apply=%region_4.0 | all-reduce | flops 131072 | bytes 786432 | tf_op jit(solution)/shard_map/psum | solution.py:26
  417.6 5.4 convolution_bitcast_fusion
  423.0 0.0 reduce-scatter.5.cloned.1.call-update
  423.0 0.0 all-gather.2.cloned.1.call-start
  423.1 76.9 %reduce-scatter.5.cloned.1.call-done = f32[128,256]{0,1:T(8,128)} async-done(((f32[4096,256]{0,1:T(8,128)}), f32[128,256]{0,1:T(8,128)}) %reduce-scatter.5.cloned.1.call-update) | async-done | bytes 131088 | tf_op jit(solution)/shard_map/reduce_scatter | solution.py:30
  500.0 1.5 convert_element_type.29
  501.5 0.0 all-gather.2.cloned.1.call-update
  501.5 0.0 all-reduce.6.cloned.1.call-start
  501.6 80.3 %all-gather.2.cloned.1.call-done = bf16[16384,256]{0,1:T(8,128)(2,1)} async-done(((bf16[128,256]{0,1:T(8,128)(2,1)}), bf16[16384,256]{0,1:T(8,128)(2,1)}) %all-gather.2.cloned.1.call-update) | async-done | bytes 8388624 | tf_op jit(solution)/shard_map/all_gather | solution.py:33
  581.9 11.9 %copy.13 = bf16[16384,256]{1,0:T(8,128)(2,1)} copy(bf16[16384,256]{0,1:T(8,128)(2,1)} %all-gather.2.cloned.1.call-done) | data formatting | bytes 16777216 | tf_op jit(solution)/shard_map/all_gather | solution.py:33
  593.8 6.6 gather_fusion
  600.3 6.1 fusion.10
  606.5 0.0 all-reduce.6.cloned.1.call-update
  606.5 0.7 copy.15
  607.3 68.0 %all-reduce.6.cloned.1.call-done = f32[3072,256]{1,0:T(8,128)} async-done(((f32[3072,256]{1,0:T(8,128)}), f32[3072,256]{1,0:T(8,128)}) %all-reduce.6.cloned.1.call-update) | async-done | bytes 3145744 | tf_op jit(solution)/shard_map/psum | solution.py:38
  675.3 8.5 %fusion.13 = f32[1536,256]{0,1:T(8,128)} fusion(bf16[1,3072,1536]{2,1,0:T(8,128)(2,1)} %param.8, f32[3072,256]{1,0:T(8,128)} %all-reduce.6.cloned.1.call-done, bf16[3072,256]{1,0:T(8,128)(2,1)S(1)} %all-reduce.7), kind=kOutput, calls=%fused_computation.15 | convolution fusion | flops 2418278400 | bytes 15728640 | tf_op jit(solution)/shard_map/dot_general | solution.py:40
  683.7 37.3 %all-reduce.10 = bf16[1536,256]{0,1:T(8,128)(2,1)S(1)} all-reduce(f32[1536,256]{0,1:T(8,128)} %fusion.13), channel_id=1, replica_groups=mesh['leaf'=4,'row'=4,'col'=8] {'row'}, use_global_device_ids=true, to_apply=%region_7.8 | all-reduce | flops 393216 | bytes 2359296 | tf_op jit(solution)/shard_map/psum | solution.py:43
  721.0 1.2 copy.14
  (12 shorter events, 0.1 us)
Async XLA Ops:
  7.2 1.1 copy-start
  7.2 232.2 %reduce-scatter.3.cloned.1.call-start = ((), (), s32[]{:S(2)}) async-start(), calls=%async_computation.2 | async-start | bytes 20971520 | tf_op jit(solution)/shard_map/reduce_scatter | solution.py:23
  73.1 4.1 copy-start.4
  77.2 12.3 %copy-start.3 = (bf16[128,256]{1,0:T(8,128)(2,1)S(1)}, bf16[128,256]{1,0:T(8,128)(2,1)}, u32[]{:S(2)}) copy-start(bf16[128,256]{1,0:T(8,128)(2,1)} %param.7) | copy-start | bytes 196612
  91.0 408.9 %reduce-scatter.5.cloned.1.call-start = ((), (), s32[]{:S(2)}) async-start(), calls=%async_computation.3 | async-start | bytes 4325376 | tf_op jit(solution)/shard_map/reduce_scatter | solution.py:30
  423.0 158.9 %all-gather.2.cloned.1.call-start = ((), (), s32[]{:S(2)}) async-start(), calls=%async_computation.4 | async-start | bytes 8454144 | tf_op jit(solution)/shard_map/all_gather | solution.py:33
  501.5 173.7 %all-reduce.6.cloned.1.call-start = ((), (), s32[]{:S(2)}) async-start(), calls=%async_computation.5 | async-start | bytes 6291456 | tf_op jit(solution)/shard_map/psum | solution.py:38
  600.3 6.2 copy-start.2
  675.3 46.9 %copy-start.1 = (bf16[1,1536,256]{2,1,0:T(8,128)(2,1)S(1)}, bf16[1,1536,256]{2,1,0:T(8,128)(2,1)}, u32[]{:S(2)}) copy-start(bf16[1,1536,256]{2,1,0:T(8,128)(2,1)} %param.6) | copy-start | bytes 2359300
Sparse Core Ops, SparseCore 0:
  91.2 148.1 reduce-scatter.2
  423.1 76.8 reduce-scatter.4
  503.4 78.4 all-gather.1
  606.6 68.5 all-reduce.5
where the time goes:
time: 729 us
  waiting for transfers between devices  374 us (51%)
  blocking collectives  268 us (37%)
  matrix products  35.8 us (5%)
  local copies, waits for them, and re-layouts  21.7 us (3%)
  other arithmetic  15.4 us (2%)
  between operations  13.9 us (2%)
    psum x1, blocking collectives, per_device(): reduced = lax.psum(leaf_block, ('row', 'col')).astype(jnp.bfloat16)  153 us
    reduce_scatter x1, waiting for transfers between devices, per_device(): lax.psum_scatter(dense, 'leaf', scatter_dimension=0, tiled=True)  148 us
    all_gather x1, waiting for transfers between devices, per_device(): lax.all_gather(sol_parent, ('leaf', 'row', 'col'), axis=0, tiled=True)  80.3 us
    reduce_scatter x1, waiting for transfers between devices, per_device(): lax.psum_scatter(back_part, ('row', 'col'), scatter_dimension=0, tiled=True)  76.9 us
    psum x1, waiting for transfers between devices, per_device(): coupling = lax.psum(coupling_part, 'col')  68 us
    psum x1, blocking collectives, per_device(): forward = lax.psum(leaf_part, 'col').astype(jnp.bfloat16)  56.8 us
    psum x1, blocking collectives, per_device(): sol_leaf = lax.psum(final_part, 'row').astype(jnp.bfloat16)  37.3 us
    psum x1, blocking collectives, per_device(): fwd_parent = lax.psum(parent_part, 'leaf').astype(jnp.bfloat16)  20.8 us
  transfers between devices with their start and end apart: 4, of which 4 were waited for; matrix products, arithmetic and copies ran while one was open for 0% of the time, Pallas kernels for 0%

commit v1 on v0

--- a/solution.py
+++ b/solution.py
@@ -30,7 +30,15 @@
     sol_parent = lax.psum_scatter(
         back_part, ("row", "col"), scatter_dimension=0, tiled=True
     ).astype(jnp.bfloat16)
-    whole_parent = lax.all_gather(sol_parent, ("leaf", "row", "col"), axis=0, tiled=True)
+    whole_parent = jnp.concatenate(
+        lax.all_to_all(
+            jnp.stack([sol_parent] * lax.axis_size(("leaf", "row", "col"))),
+            ("leaf", "row", "col"),
+            0,
+            0,
+        ),
+        axis=0,
+    )
     picked = jnp.take(whole_parent, row_map[0], axis=0)
     coupling_part = lax.dot_general(
         panel[0], picked, (((0,), (0,)), ((), ())), preferred_element_type=jnp.float32

time: 729 us -> 754 us (1.034)
  waiting for transfers between devices: 374 us -> 399 us
  starting transfers between devices: 0.16 us -> 8.59 us
  local copies, waits for them, and re-layouts: 21.7 us -> 13.4 us
    all_to_all x0 -> x1, waiting for transfers between devices: none -> 101 us  [per_device(): lax.all_to_all(jnp.stack([sol_parent] * lax.axis_size(('leaf', 'row', 'co...]
    all_gather x1 -> x0, waiting for transfers between devices: 80.3 us -> none  [per_device(): lax.all_gather(sol_parent, ('leaf', 'row', 'col'), axis=0, tiled=True)]
    all_gather x1 -> x0, local copies, waits for them, and re-layouts: 11.9 us -> none  [per_device(): lax.all_gather(sol_parent, ('leaf', 'row', 'col'), axis=0, tiled=True)]
    all_to_all x0 -> x1, starting transfers between devices: none -> 8.46 us  [per_device(): lax.all_to_all(jnp.stack([sol_parent] * lax.axis_size(('leaf', 'row', 'co...]
where the time goes in v1:
time: 754 us; the launch traced here: 753 us
  waiting for transfers between devices  399 us (53%)
  blocking collectives  268 us (36%)
  matrix products  35.8 us (5%)
  other arithmetic  14.8 us (2%)
  between operations  13.9 us (2%)
  local copies, waits for them, and re-layouts  13.4 us (2%)
  starting transfers between devices  8.59 us (1%)
    psum x1, blocking collectives, per_device(): reduced = lax.psum(leaf_block, ('row', 'col')).astype(jnp.bfloat16)  153 us
    reduce_scatter x1, waiting for transfers between devices, per_device(): lax.psum_scatter(dense, 'leaf', scatter_dimension=0, tiled=True)  148 us
    all_to_all x1, waiting for transfers between devices, per_device(): lax.all_to_all(jnp.stack([sol_parent] * lax.axis_size(('leaf', 'row', 'co...  101 us
    reduce_scatter x1, waiting for transfers between devices, per_device(): lax.psum_scatter(back_part, ('row', 'col'), scatter_dimension=0, tiled=True)  77 us
    psum x1, waiting for transfers between devices, per_device(): coupling = lax.psum(coupling_part, 'col')  72.9 us
    psum x1, blocking collectives, per_device(): forward = lax.psum(leaf_part, 'col').astype(jnp.bfloat16)  56.8 us
    psum x1, blocking collectives, per_device(): sol_leaf = lax.psum(final_part, 'row').astype(jnp.bfloat16)  37.3 us
    psum x1, blocking collectives, per_device(): fwd_parent = lax.psum(parent_part, 'leaf').astype(jnp.bfloat16)  20.8 us
  transfers between devices with their start and end apart: 4, of which 4 were waited for; matrix products, arithmetic and copies ran while one was open for 0% of the time, Pallas kernels for 0%

profile of v1, /device:TPU:0, one launch (start us, length us, event | category | flops | bytes accessed | tf_op | source)
XLA Modules:
  0.0 753.4 jit_solution(13089499741149038127)
XLA Ops:
  7.2 0.0 copy-start
  7.2 0.0 reduce-scatter.3.cloned.1.call-start
  7.2 1.1 copy-done
  8.3 8.0 %fusion.2 = f32[3072,256]{1,0:T(8,128)} fusion(bf16[1,3072,1536]{2,1,0:T(8,128)(2,1)} %param.8, bf16[1,1536,256]{2,1,0:T(8,128)(2,1)S(1)} %copy-done), kind=kOutput, calls=%fused_computation.4 | convolution fusion | flops 2415919104 | bytes 13369344 | tf_op jit(solution)/shard_map/dot_general | solution.py:19
  16.3 56.8 %all-reduce.7 = bf16[3072,256]{1,0:T(8,128)(2,1)S(1)} all-reduce(f32[3072,256]{1,0:T(8,128)} %fusion.2), channel_id=1, replica_groups=mesh['leaf'=4,'row'=4,'col'=8] {'col'}, use_global_device_ids=true, to_apply=%region_0.0 | all-reduce | flops 786432 | bytes 4718592 | tf_op jit(solution)/shard_map/psum | solution.py:20
  73.1 3.8 fusion.21
  76.9 0.3 copy.12
  77.2 12.3 %scatter_custom_fusion = f32[16384,256]{1,0:T(8,128)} fusion(s32[768]{0:T(1024)S(1)} %fusion.34, f32[768,256]{1,0:T(8,128)S(1)} %copy.12, f32[]{:T(128)} %constant.14.clone.1), kind=kCustom, calls=%fused_computation.6 | custom fusion | flops 196608 | bytes 16777220 | tf_op jit(solution)/shard_map/scatter-add | solution.py:10
  89.5 1.6 add_dynamic-update-slice_fusion
  91.0 0.0 reduce-scatter.3.cloned.1.call-update
  91.0 0.0 reduce-scatter.5.cloned.1.call-start
  91.1 148.2 %reduce-scatter.3.cloned.1.call-done = f32[4096,256]{1,0:T(8,128)} async-done(((f32[16384,256]{1,0:T(8,128)}), f32[4096,256]{1,0:T(8,128)}) %reduce-scatter.3.cloned.1.call-update) | async-done | bytes 4194320 | tf_op jit(solution)/shard_map/reduce_scatter | solution.py:23
  239.3 153.3 %all-reduce.8 = bf16[4096,256]{1,0:T(8,128)(2,1)} all-reduce(f32[4096,256]{1,0:T(8,128)} %reduce-scatter.3.cloned.1.call-done), channel_id=1, replica_groups=mesh['leaf'=4,'row'=4,'col'=8] {'row','col'}, use_global_device_ids=true, to_apply=%region_3.0 | all-reduce | flops 1048576 | bytes 6291456 | tf_op jit(solution)/shard_map/psum | solution.py:24
  392.6 4.1 fusion.24
  396.8 20.8 %all-reduce.9 = bf16[512,256]{0,1:T(8,128)(2,1)S(1)} all-reduce(f32[512,256]{0,1:T(8,128)S(1)} %fusion.24), channel_id=1, replica_groups=mesh['leaf'=4,'row'=4,'col'=8] {'leaf'}, use_global_device_ids=true, to_apply=%region_4.0 | all-reduce | flops 131072 | bytes 786432 | tf_op jit(solution)/shard_map/psum | solution.py:26
  417.6 5.4 convolution_bitcast_fusion
  423.0 0.0 reduce-scatter.5.cloned.1.call-update
  423.0 77.0 %reduce-scatter.5.cloned.1.call-done = f32[128,256]{0,1:T(8,128)} async-done(((f32[4096,256]{0,1:T(8,128)}), f32[128,256]{0,1:T(8,128)}) %reduce-scatter.5.cloned.1.call-update) | async-done | bytes 131088 | tf_op jit(solution)/shard_map/reduce_scatter | solution.py:30
  500.0 0.9 convert_element_type.29
  500.9 0.1 copy.13
  501.0 0.0 copy-start.2
  501.0 4.3 stack.2
  505.3 8.5 %all-to-all-start = ((bf16[128,128,256]{2,1,0:T(8,128)(2,1)}), bf16[128,128,256]{2,1,0:T(8,128)(2,1)}, u32[]{:S(2)}, u32[]{:S(2)}) async-start(bf16[128,128,256]{2,1,0:T(8,128)(2,1)} %stack.2), calls=%async_computation.2 | async-start | bytes 16777216 | tf_op jit(solution)/shard_map/all_to_all | solution.py:34
  513.7 0.0 all-reduce.6.cloned.1.call-start
  513.8 100.6 %all-to-all-done = bf16[128,128,256]{2,1,0:T(8,128)(2,1)} async-done(((bf16[128,128,256]{2,1,0:T(8,128)(2,1)}), bf16[128,128,256]{2,1,0:T(8,128)(2,1)}, u32[]{:S(2)}, u32[]{:S(2)}) %all-to-all-start) | async-done | bytes 8388640 | tf_op jit(solution)/shard_map/all_to_all | solution.py:34
  614.4 6.6 gather_fusion
  621.0 6.1 fusion.10
  627.1 0.0 all-reduce.6.cloned.1.call-update
  627.1 72.9 %all-reduce.6.cloned.1.call-done = f32[3072,256]{1,0:T(8,128)} async-done(((f32[3072,256]{1,0:T(8,128)}), f32[3072,256]{1,0:T(8,128)}) %all-reduce.6.cloned.1.call-update) | async-done | bytes 3145744 | tf_op jit(solution)/shard_map/psum | solution.py:46
  700.0 8.5 %fusion.13 = f32[1536,256]{0,1:T(8,128)} fusion(bf16[1,3072,1536]{2,1,0:T(8,128)(2,1)} %param.8, f32[3072,256]{1,0:T(8,128)} %all-reduce.6.cloned.1.call-done, bf16[3072,256]{1,0:T(8,128)(2,1)S(1)} %all-reduce.7), kind=kOutput, calls=%fused_computation.15 | convolution fusion | flops 2418278400 | bytes 15728640 | tf_op jit(solution)/shard_map/dot_general | solution.py:48
  708.4 37.3 %all-reduce.10 = bf16[1536,256]{0,1:T(8,128)(2,1)S(1)} all-reduce(f32[1536,256]{0,1:T(8,128)} %fusion.13), channel_id=1, replica_groups=mesh['leaf'=4,'row'=4,'col'=8] {'row'}, use_global_device_ids=true, to_apply=%region_7.8 | all-reduce | flops 393216 | bytes 2359296 | tf_op jit(solution)/shard_map/psum | solution.py:51
  745.7 1.2 copy.14
  (11 shorter events, 0.1 us)
Async XLA Ops:
  7.2 1.1 copy-start
  7.2 232.2 %reduce-scatter.3.cloned.1.call-start = ((), (), s32[]{:S(2)}) async-start(), calls=%async_computation.3 | async-start | bytes 20971520 | tf_op jit(solution)/shard_map/reduce_scatter | solution.py:23
  73.1 4.1 copy-start.4
  77.2 12.3 %copy-start.3 = (bf16[128,256]{1,0:T(8,128)(2,1)S(1)}, bf16[128,256]{1,0:T(8,128)(2,1)}, u32[]{:S(2)}) copy-start(bf16[128,256]{1,0:T(8,128)(2,1)} %param.7) | copy-start | bytes 196612
  91.0 408.9 %reduce-scatter.5.cloned.1.call-start = ((), (), s32[]{:S(2)}) async-start(), calls=%async_computation.4 | async-start | bytes 4325376 | tf_op jit(solution)/shard_map/reduce_scatter | solution.py:30
  501.0 4.3 copy-start.2
  505.3 109.1 %all-to-all-start = ((bf16[128,128,256]{2,1,0:T(8,128)(2,1)}), bf16[128,128,256]{2,1,0:T(8,128)(2,1)}, u32[]{:S(2)}, u32[]{:S(2)}) async-start(bf16[128,128,256]{2,1,0:T(8,128)(2,1)} %stack.2), calls=%async_computation.2 | async-start | bytes 16777216 | tf_op jit(solution)/shard_map/all_to_all | solution.py:34
  513.7 186.2 %all-reduce.6.cloned.1.call-start = ((), (), s32[]{:S(2)}) async-start(), calls=%async_computation.5 | async-start | bytes 6291456 | tf_op jit(solution)/shard_map/psum | solution.py:46
  700.0 46.9 %copy-start.1 = (bf16[1,1536,256]{2,1,0:T(8,128)(2,1)S(1)}, bf16[1,1536,256]{2,1,0:T(8,128)(2,1)}, u32[]{:S(2)}) copy-start(bf16[1,1536,256]{2,1,0:T(8,128)(2,1)} %param.6) | copy-start | bytes 2359300
Sparse Core Ops, SparseCore 0:
  91.2 148.1 reduce-scatter.2
  423.1 76.8 reduce-scatter.4
  627.2 72.7 all-reduce.5
